TPU v7x, 32 devices: a whole 2x2x4 slice. The times are simulated.
32 devices in a mesh: fsdp: 8 (over y, x, core), shard: 4 (over z).
Axes of the slice: x: 2, y: 2, z: 4, core: 2. Of those that a mesh axis runs over, the one named last changes fastest.
Arguments:
- tokens: bfloat16 [4096, 1024], P(('fsdp', 'shard')), may hold values from -6 to 6
- cotangent: bfloat16 [4096, 1024], P(('fsdp', 'shard')), may hold values from -6 to 6
- starts: int32 [4096], P(('fsdp', 'shard')), may hold values from 0 to 127, as said below
- counts: int32 [32], P(('fsdp', 'shard')), may hold values from 64 to 128, as said below
- attn_gain: bfloat16 [4, 256], P('shard', 'fsdp'), may hold values from 0.5 to 1.5
- attn_shift: bfloat16 [4, 256], P('shard', 'fsdp'), may hold values from -1.75 to 1.75
- w_qkv: bfloat16 [1024, 3, 1024], P('fsdp', None, 'shard'), may hold values from -0.1875 to 0.1875
- query_bias: bfloat16 [4, 256], P('shard', 'fsdp'), may hold values from -1.75 to 1.75
- value_bias: bfloat16 [4, 256], P('shard', 'fsdp'), may hold values from -1.75 to 1.75
- w_proj: bfloat16 [1024, 1024], P('shard', 'fsdp'), may hold values from -0.75 to 0.75
- proj_bias: bfloat16 [4, 256], P('shard', 'fsdp'), may hold values from -1.75 to 1.75
- mlp_gain: bfloat16 [4, 256], P('shard', 'fsdp'), may hold values from 0.5 to 1.5
- mlp_shift: bfloat16 [4, 256], P('shard', 'fsdp'), may hold values from -1.75 to 1.75
- w_up: bfloat16 [1024, 4096], P('fsdp', 'shard'), may hold values from -0.1875 to 0.1875
- up_bias: bfloat16 [4, 1024], P('shard', 'fsdp'), may hold values from -1.75 to 1.75
- w_down: bfloat16 [4096, 1024], P('shard', 'fsdp'), may hold values from -0.375 to 0.375
- down_bias: bfloat16 [4, 256], P('shard', 'fsdp'), may hold values from -1.75 to 1.75
Outputs:
- block_out: bfloat16 [4096, 1024], P(('fsdp', 'shard'))
- grad_tokens: float32 [4096, 1024], P(('fsdp', 'shard'))
- grad_attn_gain: float32 [4, 256], P('shard', 'fsdp')
- grad_attn_shift: float32 [4, 256], P('shard', 'fsdp')
- grad_w_qkv: float32 [1024, 3, 1024], P('fsdp', None, 'shard')
- grad_query_bias: float32 [4, 256], P('shard', 'fsdp')
- grad_value_bias: float32 [4, 256], P('shard', 'fsdp')
- grad_w_proj: float32 [1024, 1024], P('shard', 'fsdp')
- grad_proj_bias: float32 [4, 256], P('shard', 'fsdp')
- grad_mlp_gain: float32 [4, 256], P('shard', 'fsdp')
- grad_mlp_shift: float32 [4, 256], P('shard', 'fsdp')
- grad_w_up: float32 [1024, 4096], P('fsdp', 'shard')
- grad_up_bias: float32 [4, 1024], P('shard', 'fsdp')
- grad_w_down: float32 [4096, 1024], P('shard', 'fsdp')
- grad_down_bias: float32 [4, 256], P('shard', 'fsdp')
Inputs may be any that keep to these rules, and one draw needn't show every extreme that they name: starts[s] is the index, inside the block of 128 slots that holds slot s, of the first slot of s's sequence; a sequence's slots are consecutive in one block and never cross blocks; slots at or past the block's live count start themselves; in every draw some block holds one sequence over all 128 slots. The live slots are the first counts[b] of block b; some block is full in every draw.
All inputs are finite; a program needn't handle non-finite values.
Results may differ from a plain program's by a relative error of at most 0.012.
Values may be sent and summed in bfloat16 or wider, within the bound.
No kernel may reach another device: no remote copies, remote signals or barrier semaphores. Data moves between devices by JAX's collectives and lax.ppermute only.
A program may use at most 128 MiB of HBM per device.

v0:
```python
import jax
import jax.numpy as jnp
from jax import lax
from jax.sharding import PartitionSpec as P

HEAD_DIM = 64
NORM_EPS = 1e-05
NEG_FILL = -1e30


def layer_norm(inputs, norm_gain, norm_shift):
    center = inputs - jnp.mean(inputs, axis=-1, keepdims=True)
    variance = jnp.mean(center * center, axis=-1, keepdims=True)
    return center * lax.rsqrt(variance + NORM_EPS) * norm_gain + norm_shift


def gelu_tanh(values):
    return jax.nn.gelu(values, approximate=True)


def split_heads(qkv_full, quarter, slot_count):
    row_count = qkv_full.shape[0]
    grid = (row_count // slot_count, slot_count, quarter // HEAD_DIM, HEAD_DIM)
    query_part = qkv_full[:, :quarter].reshape(grid)
    key_part = qkv_full[:, quarter : 2 * quarter].reshape(grid)
    value_part = qkv_full[:, 2 * quarter :].reshape(grid)
    return (query_part, key_part, value_part)


def score_blocks(query_part, key_part, starts_grid):
    scores = jnp.einsum("bqhd,bkhd->bhqk", query_part, key_part, preferred_element_type=jnp.float32)
    scores = scores * HEAD_DIM ** (-0.5)
    positions = jnp.arange(scores.shape[2], dtype=jnp.int32)
    visible = (positions[None, None, :] >= starts_grid[:, :, None]) & (
        positions[None, None, :] <= positions[None, :, None]
    )
    return jnp.where(visible[:, None], scores, NEG_FILL)


def collect(params):
    over = (
        lax.all_gather(params[0], "fsdp", axis=1, tiled=True),
        lax.all_gather(params[1], "fsdp", axis=1, tiled=True),
        lax.all_gather(params[2], "fsdp", axis=0, tiled=True),
        lax.all_gather(params[3], "fsdp", axis=1, tiled=True),
        lax.all_gather(params[4], "fsdp", axis=1, tiled=True),
        lax.all_gather(params[5], "fsdp", axis=1, tiled=True),
        lax.all_gather(params[6], "fsdp", axis=1, tiled=True),
        lax.all_gather(params[7], "fsdp", axis=1, tiled=True),
        lax.all_gather(params[8], "fsdp", axis=1, tiled=True),
        lax.all_gather(params[9], "fsdp", axis=0, tiled=True),
        lax.all_gather(params[10], "fsdp", axis=1, tiled=True),
        lax.all_gather(params[11], "fsdp", axis=1, tiled=True),
        lax.all_gather(params[12], "fsdp", axis=1, tiled=True),
    )
    vectors = (
        lax.all_gather(over[0], "shard", axis=0, tiled=True),
        lax.all_gather(over[1], "shard", axis=0, tiled=True),
        lax.all_gather(over[6], "shard", axis=0, tiled=True),
        lax.all_gather(over[7], "shard", axis=0, tiled=True),
        lax.all_gather(over[8], "shard", axis=0, tiled=True),
        lax.all_gather(over[12], "shard", axis=0, tiled=True),
    )
    full = (
        vectors[0].reshape(-1),
        vectors[1].reshape(-1),
        over[2],
        over[3].reshape(-1),
        over[4].reshape(-1),
        over[5],
        vectors[2].reshape(-1),
        vectors[3].reshape(-1),
        vectors[4].reshape(-1),
        over[9],
        over[10].reshape(-1),
        over[11],
        vectors[5].reshape(-1),
    )
    return full


def spread(grads, shard_count):
    (
        g_attn_gain,
        g_attn_shift,
        g_qkv,
        g_query_bias,
        g_value_bias,
        g_proj,
        g_proj_bias,
        g_mlp_gain,
        g_mlp_shift,
        g_up,
        g_up_bias,
        g_down,
        g_down_bias,
    ) = grads
    summed = (
        lax.psum_scatter(
            g_attn_gain.reshape(shard_count, -1), "shard", scatter_dimension=0, tiled=True
        ),
        lax.psum_scatter(
            g_attn_shift.reshape(shard_count, -1), "shard", scatter_dimension=0, tiled=True
        ),
        lax.psum_scatter(
            g_proj_bias.reshape(shard_count, -1), "shard", scatter_dimension=0, tiled=True
        ),
        lax.psum_scatter(
            g_mlp_gain.reshape(shard_count, -1), "shard", scatter_dimension=0, tiled=True
        ),
        lax.psum_scatter(
            g_mlp_shift.reshape(shard_count, -1), "shard", scatter_dimension=0, tiled=True
        ),
        lax.psum_scatter(
            g_down_bias.reshape(shard_count, -1), "shard", scatter_dimension=0, tiled=True
        ),
    )
    pieces = (
        summed[0],
        summed[1],
        g_qkv,
        g_query_bias.reshape(1, -1),
        g_value_bias.reshape(1, -1),
        g_proj,
        summed[2],
        summed[3],
        summed[4],
        g_up,
        g_up_bias.reshape(1, -1),
        g_down,
        summed[5],
    )
    owned = (
        lax.psum_scatter(pieces[0], "fsdp", scatter_dimension=1, tiled=True),
        lax.psum_scatter(pieces[1], "fsdp", scatter_dimension=1, tiled=True),
        lax.psum_scatter(pieces[2], "fsdp", scatter_dimension=0, tiled=True),
        lax.psum_scatter(pieces[3], "fsdp", scatter_dimension=1, tiled=True),
        lax.psum_scatter(pieces[4], "fsdp", scatter_dimension=1, tiled=True),
        lax.psum_scatter(pieces[5], "fsdp", scatter_dimension=1, tiled=True),
        lax.psum_scatter(pieces[6], "fsdp", scatter_dimension=1, tiled=True),
        lax.psum_scatter(pieces[7], "fsdp", scatter_dimension=1, tiled=True),
        lax.psum_scatter(pieces[8], "fsdp", scatter_dimension=1, tiled=True),
        lax.psum_scatter(pieces[9], "fsdp", scatter_dimension=0, tiled=True),
        lax.psum_scatter(pieces[10], "fsdp", scatter_dimension=1, tiled=True),
        lax.psum_scatter(pieces[11], "fsdp", scatter_dimension=1, tiled=True),
        lax.psum_scatter(pieces[12], "fsdp", scatter_dimension=1, tiled=True),
    )
    return owned


def forward_pass(full, tokens, starts, live):
    (
        attn_gain,
        attn_shift,
        w_qkv,
        query_bias,
        value_bias,
        w_proj,
        proj_bias,
        mlp_gain,
        mlp_shift,
        w_up,
        up_bias,
        w_down,
        down_bias,
    ) = full
    slot_count = tokens.shape[0]
    width = tokens.shape[1]
    tokens_wide = tokens.astype(jnp.float32)
    normed_attn = layer_norm(
        tokens_wide, attn_gain.astype(jnp.float32), attn_shift.astype(jnp.float32)
    )
    act_attn = normed_attn.astype(jnp.bfloat16)
    act_rows, start_rows = (
        lax.all_gather(act_attn, "shard", axis=0, tiled=True),
        lax.all_gather(starts, "shard", axis=0, tiled=True),
    )
    quarter = w_qkv.shape[2]
    row_count = act_rows.shape[0]
    qkv_bias = jnp.concatenate([query_bias, jnp.zeros_like(query_bias), value_bias]).astype(
        jnp.float32
    )
    qkv_full = (
        jnp.dot(act_rows, w_qkv.reshape(width, 3 * quarter), preferred_element_type=jnp.float32)
        + qkv_bias
    ).astype(jnp.bfloat16)
    query_part, key_part, value_part = split_heads(qkv_full, quarter, slot_count)
    starts_grid = start_rows.reshape(row_count // slot_count, slot_count)
    scores = score_blocks(query_part, key_part, starts_grid)
    row_max = jnp.max(scores, axis=-1, keepdims=True)
    log_total = row_max + jnp.log(jnp.sum(jnp.exp(scores - row_max), axis=-1, keepdims=True))
    probs_low = jnp.exp(scores - log_total).astype(jnp.bfloat16)
    mixed = jnp.einsum("bhqk,bkhd->bqhd", probs_low, value_part, preferred_element_type=jnp.float32)
    mixed = mixed.reshape(row_count, quarter).astype(jnp.bfloat16)
    attn_term = lax.psum_scatter(
        jnp.dot(mixed, w_proj, preferred_element_type=jnp.float32),
        "shard",
        scatter_dimension=0,
        tiled=True,
    )
    hidden_one = tokens_wide + attn_term + proj_bias.astype(jnp.float32)
    normed_mlp = layer_norm(hidden_one, mlp_gain.astype(jnp.float32), mlp_shift.astype(jnp.float32))
    act_mlp = normed_mlp.astype(jnp.bfloat16)
    mlp_inputs = lax.all_gather(act_mlp, "shard", axis=0, tiled=True)
    pre_act = jnp.dot(mlp_inputs, w_up, preferred_element_type=jnp.float32) + up_bias.astype(
        jnp.float32
    )
    act_up = gelu_tanh(pre_act).astype(jnp.bfloat16)
    mlp_term = lax.psum_scatter(
        jnp.dot(act_up, w_down, preferred_element_type=jnp.float32),
        "shard",
        scatter_dimension=0,
        tiled=True,
    )
    block_out = (hidden_one + mlp_term + down_bias.astype(jnp.float32)) * live
    saved = (
        act_rows,
        starts_grid,
        qkv_full,
        log_total,
        mixed,
        hidden_one,
        mlp_inputs,
        pre_act,
        act_up,
    )
    return (block_out.astype(jnp.bfloat16), saved)


def backward_pass(full, saved, tokens, cotangent, live):
    (
        attn_gain,
        attn_shift,
        w_qkv,
        query_bias,
        value_bias,
        w_proj,
        proj_bias,
        mlp_gain,
        mlp_shift,
        w_up,
        up_bias,
        w_down,
        down_bias,
    ) = full
    act_rows, starts_grid, qkv_full, log_total, mixed, hidden_one, mlp_inputs, pre_act, act_up = (
        saved
    )
    slot_count = tokens.shape[0]
    width = tokens.shape[1]
    quarter = w_qkv.shape[2]
    row_count = act_rows.shape[0]
    tokens_wide = tokens.astype(jnp.float32)
    grad_out = cotangent.astype(jnp.float32) * live
    grad_low = grad_out.astype(jnp.bfloat16)
    grad_low_rows = lax.all_gather(grad_low, "shard", axis=0, tiled=True)
    g_down = jnp.dot(act_up.T, grad_low_rows, preferred_element_type=jnp.float32)
    g_down_bias = jnp.sum(grad_out, axis=0)
    grad_act = jnp.dot(grad_low_rows, w_down.T, preferred_element_type=jnp.float32)
    gelu_value, gelu_back = jax.vjp(gelu_tanh, pre_act)
    (grad_pre,) = gelu_back(grad_act)
    grad_pre_low = grad_pre.astype(jnp.bfloat16)
    g_up = jnp.dot(mlp_inputs.T, grad_pre_low, preferred_element_type=jnp.float32)
    g_up_bias = jnp.sum(grad_pre, axis=0)
    grad_normed = lax.psum_scatter(
        jnp.dot(grad_pre_low, w_up.T, preferred_element_type=jnp.float32),
        "shard",
        scatter_dimension=0,
        tiled=True,
    )
    norm_value, norm_back = jax.vjp(
        layer_norm, hidden_one, mlp_gain.astype(jnp.float32), mlp_shift.astype(jnp.float32)
    )
    grad_hidden_part, g_mlp_gain, g_mlp_shift = norm_back(grad_normed)
    grad_hidden = grad_out + grad_hidden_part
    grad_hidden_low = grad_hidden.astype(jnp.bfloat16)
    hidden_rows = lax.all_gather(grad_hidden_low, "shard", axis=0, tiled=True)
    g_proj = jnp.dot(mixed.T, hidden_rows, preferred_element_type=jnp.float32)
    g_proj_bias = jnp.sum(grad_hidden, axis=0)
    grad_mixed = jnp.dot(hidden_rows, w_proj.T, preferred_element_type=jnp.float32).astype(
        jnp.bfloat16
    )
    grad_mixed = grad_mixed.reshape(
        row_count // slot_count, slot_count, quarter // HEAD_DIM, HEAD_DIM
    )
    query_part, key_part, value_part = split_heads(qkv_full, quarter, slot_count)
    scores = score_blocks(query_part, key_part, starts_grid)
    attn_probs = jnp.exp(scores - log_total)
    probs_low = attn_probs.astype(jnp.bfloat16)
    grad_probs = jnp.einsum(
        "bqhd,bkhd->bhqk", grad_mixed, value_part, preferred_element_type=jnp.float32
    )
    grad_value = jnp.einsum(
        "bhqk,bqhd->bkhd", probs_low, grad_mixed, preferred_element_type=jnp.float32
    )
    row_dot = jnp.sum(attn_probs * grad_probs, axis=-1, keepdims=True)
    grad_scores = (attn_probs * (grad_probs - row_dot) * HEAD_DIM ** (-0.5)).astype(jnp.bfloat16)
    grad_query = jnp.einsum(
        "bhqk,bkhd->bqhd", grad_scores, key_part, preferred_element_type=jnp.float32
    )
    grad_key = jnp.einsum(
        "bhqk,bqhd->bkhd", grad_scores, query_part, preferred_element_type=jnp.float32
    )
    grad_query = grad_query.reshape(row_count, quarter)
    grad_key = grad_key.reshape(row_count, quarter)
    grad_value = grad_value.reshape(row_count, quarter)
    g_query_bias = jnp.sum(grad_query, axis=0)
    g_value_bias = jnp.sum(grad_value, axis=0)
    grad_qkv_low = jnp.concatenate([grad_query, grad_key, grad_value], axis=1).astype(jnp.bfloat16)
    g_qkv = jnp.dot(act_rows.T, grad_qkv_low, preferred_element_type=jnp.float32).reshape(
        width, 3, quarter
    )
    qkv_matrix = w_qkv.reshape(width, 3 * quarter)
    grad_normed_attn = lax.psum_scatter(
        jnp.dot(grad_qkv_low, qkv_matrix.T, preferred_element_type=jnp.float32),
        "shard",
        scatter_dimension=0,
        tiled=True,
    )
    first_value, first_back = jax.vjp(
        layer_norm, tokens_wide, attn_gain.astype(jnp.float32), attn_shift.astype(jnp.float32)
    )
    grad_in_part, g_attn_gain, g_attn_shift = first_back(grad_normed_attn)
    grad_in = grad_hidden + grad_in_part
    grads = (
        g_attn_gain,
        g_attn_shift,
        g_qkv,
        g_query_bias,
        g_value_bias,
        g_proj,
        g_proj_bias,
        g_mlp_gain,
        g_mlp_shift,
        g_up,
        g_up_bias,
        g_down,
        g_down_bias,
    )
    return (grad_in, grads)


def on_device(
    tokens,
    cotangent,
    starts,
    counts,
    attn_gain,
    attn_shift,
    w_qkv,
    query_bias,
    value_bias,
    w_proj,
    proj_bias,
    mlp_gain,
    mlp_shift,
    w_up,
    up_bias,
    w_down,
    down_bias,
):
    shard_count = lax.axis_size("shard")
    params = (
        attn_gain,
        attn_shift,
        w_qkv,
        query_bias,
        value_bias,
        w_proj,
        proj_bias,
        mlp_gain,
        mlp_shift,
        w_up,
        up_bias,
        w_down,
        down_bias,
    )
    full_forward = collect(params)
    live = (jnp.arange(tokens.shape[0], dtype=jnp.int32) < counts[0]).astype(jnp.float32)[:, None]
    output_low, saved = forward_pass(full_forward, tokens, starts, live)
    full_backward = collect(params)
    grad_in, grads = backward_pass(full_backward, saved, tokens, cotangent, live)
    owned = spread(grads, shard_count)
    return (
        output_low,
        grad_in,
        owned[0],
        owned[1],
        owned[2],
        owned[3],
        owned[4],
        owned[5],
        owned[6],
        owned[7],
        owned[8],
        owned[9],
        owned[10],
        owned[11],
        owned[12],
    )


def solution(mesh):
    in_specs = (
        P(("fsdp", "shard"), None),
        P(("fsdp", "shard"), None),
        P(("fsdp", "shard")),
        P(("fsdp", "shard")),
        P("shard", "fsdp"),
        P("shard", "fsdp"),
        P("fsdp", None, "shard"),
        P("shard", "fsdp"),
        P("shard", "fsdp"),
        P("shard", "fsdp"),
        P("shard", "fsdp"),
        P("shard", "fsdp"),
        P("shard", "fsdp"),
        P("fsdp", "shard"),
        P("shard", "fsdp"),
        P("shard", "fsdp"),
        P("shard", "fsdp"),
    )
    out_specs = (
        P(("fsdp", "shard"), None),
        P(("fsdp", "shard"), None),
        P("shard", "fsdp"),
        P("shard", "fsdp"),
        P("fsdp", None, "shard"),
        P("shard", "fsdp"),
        P("shard", "fsdp"),
        P("shard", "fsdp"),
        P("shard", "fsdp"),
        P("shard", "fsdp"),
        P("shard", "fsdp"),
        P("fsdp", "shard"),
        P("shard", "fsdp"),
        P("shard", "fsdp"),
        P("shard", "fsdp"),
    )
    return jax.shard_map(
        on_device, mesh=mesh, in_specs=in_specs, out_specs=out_specs, check_vma=False
    )
```

profile of v0, /device:TPU:0, one launch (start us, length us, event | category | flops | bytes accessed | tf_op | source)
XLA Modules:
  0.0 999.4 jit_solution(1785968189932253058)
XLA Ops:
  15.9 15.1 %all-reduce.15 = (bf16[256]{0:T(256)(128)(2,1)S(1)}, bf16[256]{0:T(256)(128)(2,1)S(1)}, bf16[256]{0:T(256)(128)(2,1)S(1)}, bf16[256]{0:T(256)(128)(2,1)S(1)}, bf...) all-reduce(bf16[256]{0:T(256)(128)(2,1)S(1)} %dynamic-update-slice., ...), channel_id=1, replica_groups=mesh['fsdp'=8,'shard'=4] {'fsdp'}, use_global_device_ids=true, to_apply=%add.1 | all-reduce | flops 2048 | bytes 8192
  31.1 11.2 %all-gather = bf16[4,1,256]{2,1,0:T(2,128)(2,1)S(1)} all-gather(bf16[1,1,256]{2,1,0:T(2,128)(2,1)S(1)} %reshape.313), channel_id=1, replica_groups=mesh['fsdp'=8,'shard'=4] {'shard'}, dimensions={0}, use_global_device_ids=true | all-gather | bytes 2560 | tf_op jit(solution)/shard_map/all_gather | solution.py:57
  42.2 7.6 all-gather.1
  55.9 9.7 all-gather.2
  65.6 9.0 all_gather.89
  74.7 5.2 all-gather.15.cloned.1.call-done
  79.9 27.8 %all-gather.17.cloned.1.call-done = bf16[1024,3,256]{0,2,1:T(8,128)(2,1)} async-done(((bf16[128,3,256]{0,2,1:T(8,128)(2,1)}), bf16[1024,3,256]{0,2,1:T(8,128)(2,1)}) %all-gather.17.cloned.1.call-update) | async-done | bytes 1572880 | tf_op jit(solution)/shard_map/all_gather | solution.py:44
  107.7 2.8 add_convert_fusion
  115.7 10.9 %all-gather.3 = bf16[4,1,256]{2,1,0:T(2,128)(2,1)S(1)} all-gather(bf16[1,1,256]{2,1,0:T(2,128)(2,1)S(1)} %reshape.319), channel_id=1, replica_groups=mesh['fsdp'=8,'shard'=4] {'shard'}, dimensions={0}, use_global_device_ids=true | all-gather | bytes 2560 | tf_op jit(solution)/shard_map/all_gather | solution.py:59
  126.6 7.8 all-gather.4
  134.4 10.3 %all-gather.5 = bf16[4,1,256]{2,1,0:T(2,128)(2,1)S(1)} all-gather(bf16[1,1,256]{2,1,0:T(2,128)(2,1)S(1)} %reshape.323), channel_id=1, replica_groups=mesh['fsdp'=8,'shard'=4] {'shard'}, dimensions={0}, use_global_device_ids=true | all-gather | bytes 2560 | tf_op jit(solution)/shard_map/all_gather | solution.py:61
  144.8 14.4 %reduce-scatter.36.cloned.1.call-done = f32[128,1024]{1,0:T(8,128)} async-done(((f32[512,1024]{1,0:T(8,128)}), f32[128,1024]{1,0:T(8,128)}) %reduce-scatter.36.cloned.1.call-update) | async-done | bytes 524304 | tf_op jit(solution)/shard_map/reduce_scatter | solution.py:195
  163.9 8.9 all_gather.98
  172.8 15.5 %all-gather.21.cloned.1.call-done = bf16[1024,1024]{1,0:T(8,128)(2,1)} async-done(((bf16[128,1024]{1,0:T(8,128)(2,1)}), bf16[1024,1024]{1,0:T(8,128)(2,1)}) %all-gather.21.cloned.1.call-update) | async-done | bytes 2097168 | tf_op jit(solution)/shard_map/all_gather | solution.py:51
  188.3 30.0 %all-gather.19.cloned.1.call-done = bf16[512,1024]{1,0:T(8,128)(2,1)} async-done(((bf16[128,1024]{1,0:T(8,128)(2,1)}), bf16[512,1024]{1,0:T(8,128)(2,1)}) %all-gather.19.cloned.1.call-update) | async-done | bytes 1048592 | tf_op jit(solution)/shard_map/all_gather | solution.py:204
  218.3 4.5 fusion.75
  222.8 25.0 %all-gather.25.cloned.1.call-done = bf16[512,1024]{1,0:T(8,128)(2,1)} async-done(((bf16[128,1024]{1,0:T(8,128)(2,1)}), bf16[512,1024]{1,0:T(8,128)(2,1)}) %all-gather.25.cloned.1.call-update) | async-done | bytes 1048592 | tf_op jit(solution)/shard_map/all_gather | solution.py:256
  247.9 29.8 %all-gather.23.cloned.1.call-done = bf16[1024,1024]{1,0:T(8,128)(2,1)} async-done(((bf16[1024,128]{1,0:T(8,128)(2,1)}), bf16[1024,1024]{1,0:T(8,128)(2,1)}) %all-gather.23.cloned.1.call-update) | async-done | bytes 2097168 | tf_op jit(solution)/shard_map/all_gather | solution.py:53
  277.6 5.2 fusion.64
  283.8 2.6 fusion.33
  286.5 5.1 fusion.62
  291.7 11.2 %all-gather.6 = bf16[4,1,256]{2,1,0:T(2,128)(2,1)S(1)} all-gather(bf16[1,1,256]{2,1,0:T(2,128)(2,1)S(1)} %reshape.325), channel_id=1, replica_groups=mesh['fsdp'=8,'shard'=4] {'shard'}, dimensions={0}, use_global_device_ids=true | all-gather | bytes 2560 | tf_op jit(solution)/shard_map/all_gather | solution.py:62
  302.8 27.7 %reduce-scatter.40.cloned.1.call-done = f32[128,1024]{1,0:T(8,128)} async-done(((f32[512,1024]{1,0:T(8,128)}), f32[128,1024]{1,0:T(8,128)}) %reduce-scatter.40.cloned.1.call-update) | async-done | bytes 524304 | tf_op jit(solution)/shard_map/reduce_scatter | solution.py:265
  331.9 44.2 %reduce-scatter.38.cloned.1.call-done = f32[128,1024]{1,0:T(8,128)} async-done(((f32[512,1024]{1,0:T(8,128)}), f32[128,1024]{1,0:T(8,128)}) %reduce-scatter.38.cloned.1.call-update) | async-done | bytes 524304 | tf_op jit(solution)/shard_map/reduce_scatter | solution.py:209
  376.0 2.1 fusion.66
  379.1 27.4 %all-gather.27.cloned.1.call-done = bf16[512,1024]{1,0:T(8,128)(2,1)} async-done(((bf16[128,1024]{1,0:T(8,128)(2,1)}), bf16[512,1024]{1,0:T(8,128)(2,1)}) %all-gather.27.cloned.1.call-update) | async-done | bytes 1048592 | tf_op jit(solution)/shard_map/all_gather | solution.py:277
  411.4 2.2 fusion.13
  413.6 2.2 fusion.71
  417.2 2.3 fusion.77
  423.1 40.0 %reduce-scatter.42.cloned.1.call-done = f32[128,1024]{1,0:T(8,128)} async-done(((f32[512,1024]{1,0:T(8,128)}), f32[128,1024]{1,0:T(8,128)}) %reduce-scatter.42.cloned.1.call-update) | async-done | bytes 524304 | tf_op jit(solution)/shard_map/reduce_scatter | solution.py:314
  465.8 2.3 fusion.35
  468.1 17.1 %all-reduce.14 = (f32[4,256]{1,0:T(4,128)S(1)}, f32[4,256]{1,0:T(4,128)S(1)}, f32[4,256]{1,0:T(4,128)S(1)}, f32[4,256]{1,0:T(4,128)S(1)}, f32[4,256]{1,0:T(4,128)S(1)}, /*index=5*/f32[4,256]{1,0:T(4,128)S(1)}) all-reduce(f32[4,256]{1,0:T(4,128)S(1)} %reshape.272, ...), channel_id=6, replica_groups=mesh['fsdp'=8,'shard'=4] {'shard'}, use_global_device_ids=true, to_apply=%region_16.17.clone | all-reduce | flops 6144 | bytes 49152
  492.4 4.4 fusion.31
  498.8 3.6 fusion.61
  505.0 2.4 fusion.78
  507.5 2.5 copy.88
  511.4 24.8 %reduce-scatter.58.cloned.1.call-done = f32[32,1]{1,0:T(8,128)} async-done(((f32[256,1]{1,0:T(8,128)}), f32[32,1]{1,0:T(8,128)}) %reduce-scatter.58.cloned.1.call-update) | async-done | bytes 144
  537.5 35.0 %reduce-scatter.56.cloned.1.call-done = f32[32,1]{1,0:T(8,128)} async-done(((f32[256,1]{1,0:T(8,128)}), f32[32,1]{1,0:T(8,128)}) %reduce-scatter.56.cloned.1.call-update) | async-done | bytes 144
  573.8 35.2 %reduce-scatter.64.cloned.1.call-done = f32[32,1]{1,0:T(8,128)} async-done(((f32[256,1]{1,0:T(8,128)}), f32[32,1]{1,0:T(8,128)}) %reduce-scatter.64.cloned.1.call-update) | async-done | bytes 144
  610.3 35.0 %reduce-scatter.68.cloned.1.call-done = f32[32,1]{1,0:T(8,128)} async-done(((f32[256,1]{1,0:T(8,128)}), f32[32,1]{1,0:T(8,128)}) %reduce-scatter.68.cloned.1.call-update) | async-done | bytes 144
  646.6 35.2 %reduce-scatter.60.cloned.1.call-done = f32[32,1]{1,0:T(8,128)} async-done(((f32[256,1]{1,0:T(8,128)}), f32[32,1]{1,0:T(8,128)}) %reduce-scatter.60.cloned.1.call-update) | async-done | bytes 144
  683.1 35.0 %reduce-scatter.62.cloned.1.call-done = f32[32,1]{1,0:T(8,128)} async-done(((f32[256,1]{1,0:T(8,128)}), f32[32,1]{1,0:T(8,128)}) %reduce-scatter.62.cloned.1.call-update) | async-done | bytes 144
  719.4 35.3 %reduce-scatter.52.cloned.1.call-done = f32[32,1]{1,0:T(8,128)} async-done(((f32[256,1]{1,0:T(8,128)}), f32[32,1]{1,0:T(8,128)}) %reduce-scatter.52.cloned.1.call-update) | async-done | bytes 144
  756.0 35.0 %reduce-scatter.54.cloned.1.call-done = f32[32,1]{1,0:T(8,128)} async-done(((f32[256,1]{1,0:T(8,128)}), f32[32,1]{1,0:T(8,128)}) %reduce-scatter.54.cloned.1.call-update) | async-done | bytes 144
  792.3 54.4 %reduce-scatter.48.cloned.1.call-done = f32[128,1024]{1,0:T(8,128)} async-done(((f32[1024,1024]{1,0:T(8,128)}), f32[128,1024]{1,0:T(8,128)}) %reduce-scatter.48.cloned.1.call-update) | async-done | bytes 524304 | tf_op jit(solution)/shard_map/reduce_scatter | solution.py:143
  846.6 55.3 %reduce-scatter.50.cloned.1.call-done = f32[1024,128]{1,0:T(8,128)} async-done(((f32[1024,1024]{1,0:T(8,128)}), f32[1024,128]{1,0:T(8,128)}) %reduce-scatter.50.cloned.1.call-update) | async-done | bytes 524304 | tf_op jit(solution)/shard_map/reduce_scatter | solution.py:145
  901.9 40.2 %reduce-scatter.46.cloned.1.call-done = f32[256,128]{1,0:T(8,128)} async-done(((f32[256,1024]{1,0:T(8,128)}), f32[256,128]{1,0:T(8,128)}) %reduce-scatter.46.cloned.1.call-update) | async-done | bytes 131088 | tf_op jit(solution)/shard_map/reduce_scatter | solution.py:139
  942.1 50.5 %reduce-scatter.44.cloned.1.call-done = f32[128,3,256]{2,0,1:T(8,128)} async-done(((f32[1024,3,256]{2,0,1:T(8,128)}), f32[128,3,256]{2,0,1:T(8,128)}) %reduce-scatter.44.cloned.1.call-update) | async-done | bytes 393232 | tf_op jit(solution)/shard_map/reduce_scatter | solution.py:136
  (195 shorter events, 62.4 us)
Async XLA Ops:
  7.2 58.4 %copy-start.12 = (bf16[256,128]{1,0:T(8,128)(2,1)S(1)}, bf16[256,128]{1,0:T(8,128)(2,1)}, u32[]{:S(2)}) copy-start(bf16[256,128]{1,0:T(8,128)(2,1)} %param.26) | copy-start | bytes 196612
  7.2 72.7 %all-gather.15.cloned.1.call-start = ((), (), s32[]{:S(2)}) async-start(), calls=%async_computation.17 | async-start | bytes 1310720 | tf_op jit(solution)/shard_map/all_gather | solution.py:175
  54.0 53.7 %all-gather.17.cloned.1.call-start = ((), (), s32[]{:S(2)}) async-start(), calls=%async_computation.18 | async-start | bytes 1769472 | tf_op jit(solution)/shard_map/all_gather | solution.py:44
  55.8 103.4 %reduce-scatter.36.cloned.1.call-start = ((), (), s32[]{:S(2)}) async-start(), calls=%async_computation.19 | async-start | bytes 2621440 | tf_op jit(solution)/shard_map/reduce_scatter | solution.py:195
  74.6 38.6 %copy-start.3 = (bf16[256,1024]{1,0:T(8,128)(2,1)}, bf16[256,1024]{1,0:T(8,128)(2,1)S(1)}, u32[]{:S(2)}) copy-start(bf16[256,1024]{1,0:T(8,128)(2,1)S(1)} %all_gather.89) | copy-start | bytes 1572868
  111.1 1.4 copy-start.5
  111.6 1.1 copy-start.7
  113.2 46.0 %copy-start = (bf16[128,1024]{1,0:T(8,128)(2,1)S(1)}, bf16[128,1024]{1,0:T(8,128)(2,1)}, u32[]{:S(2)}) copy-start(bf16[128,1024]{1,0:T(8,128)(2,1)} %param.17) | copy-start | bytes 786436
  115.0 47.2 %copy-start.2 = (bf16[128,1024]{1,0:T(8,128)(2,1)S(1)}, bf16[128,1024]{1,0:T(8,128)(2,1)}, u32[]{:S(2)}) copy-start(bf16[128,1024]{1,0:T(8,128)(2,1)} %param.18) | copy-start | bytes 786436
  115.0 48.8 %copy-start.13 = (bf16[1,128]{1,0:T(2,128)(2,1)S(1)}, bf16[1,128]{1,0:T(2,128)(2,1)}, u32[]{:S(2)}) copy-start(bf16[1,128]{1,0:T(2,128)(2,1)} %param.31) | copy-start | bytes 772
  115.0 73.3 %all-gather.21.cloned.1.call-start = ((), (), s32[]{:S(2)}) async-start(), calls=%async_computation.21 | async-start | bytes 2359296 | tf_op jit(solution)/shard_map/all_gather | solution.py:51
  115.6 102.7 %all-gather.19.cloned.1.call-start = ((), (), s32[]{:S(2)}) async-start(), calls=%async_computation.20 | async-start | bytes 1310720 | tf_op jit(solution)/shard_map/all_gather | solution.py:204
  161.5 86.4 %all-gather.25.cloned.1.call-start = ((), (), s32[]{:S(2)}) async-start(), calls=%async_computation.24 | async-start | bytes 1310720 | tf_op jit(solution)/shard_map/all_gather | solution.py:256
  163.1 114.6 %all-gather.23.cloned.1.call-start = ((), (), s32[]{:S(2)}) async-start(), calls=%async_computation.22 | async-start | bytes 2359296 | tf_op jit(solution)/shard_map/all_gather | solution.py:53
  163.8 166.7 %reduce-scatter.40.cloned.1.call-start = ((), (), s32[]{:S(2)}) async-start(), calls=%async_computation.25 | async-start | bytes 2621440 | tf_op jit(solution)/shard_map/reduce_scatter | solution.py:265
  277.6 6.2 copy-start.14
  282.8 1.0 copy-start.11
  286.5 89.6 %reduce-scatter.38.cloned.1.call-start = ((), (), s32[]{:S(2)}) async-start(), calls=%async_computation.23 | async-start | bytes 2621440 | tf_op jit(solution)/shard_map/reduce_scatter | solution.py:209
  291.6 114.9 %all-gather.27.cloned.1.call-start = ((), (), s32[]{:S(2)}) async-start(), calls=%async_computation.26 | async-start | bytes 1310720 | tf_op jit(solution)/shard_map/all_gather | solution.py:277
  379.1 84.0 %reduce-scatter.42.cloned.1.call-start = ((), (), s32[]{:S(2)}) async-start(), calls=%async_computation.27 | async-start | bytes 2621440 | tf_op jit(solution)/shard_map/reduce_scatter | solution.py:314
  408.8 2.6 copy-start.6
  410.0 3.5 copy-start.8
  411.4 4.4 copy-start.10
  415.8 1.4 copy-start.15
  417.2 2.4 copy-start.1
  419.6 2.1 copy-start.17
  419.6 90.4 %reduce-scatter.66.cloned.1.call-start = ((), (), s32[]{:S(2)}) async-start(), calls=%async_computation.39 | async-start | bytes 589824
  420.7 115.5 %reduce-scatter.58.cloned.1.call-start = ((), (), s32[]{:S(2)}) async-start(), calls=%async_computation.35 | async-start | bytes 147456
  421.6 150.9 %reduce-scatter.56.cloned.1.call-start = ((), (), s32[]{:S(2)}) async-start(), calls=%async_computation.34 | async-start | bytes 147456
  423.1 186.0 %reduce-scatter.64.cloned.1.call-start = ((), (), s32[]{:S(2)}) async-start(), calls=%async_computation.38 | async-start | bytes 147456
  465.8 26.6 %copy-start.4 = (bf16[512,1024]{1,0:T(8,128)(2,1)S(1)}, bf16[512,1024]{1,0:T(8,128)(2,1)}, u32[]{:S(2)}) copy-start(bf16[512,1024]{1,0:T(8,128)(2,1)} %all-gather.19.cloned.1.call-done) | copy-start | bytes 3145732
  486.7 158.6 %reduce-scatter.68.cloned.1.call-start = ((), (), s32[]{:S(2)}) async-start(), calls=%async_computation.40 | async-start | bytes 147456
  487.5 194.2 %reduce-scatter.60.cloned.1.call-start = ((), (), s32[]{:S(2)}) async-start(), calls=%async_computation.36 | async-start | bytes 147456
  489.1 229.0 %reduce-scatter.62.cloned.1.call-start = ((), (), s32[]{:S(2)}) async-start(), calls=%async_computation.37 | async-start | bytes 147456
  489.9 264.8 %reduce-scatter.52.cloned.1.call-start = ((), (), s32[]{:S(2)}) async-start(), calls=%async_computation.32 | async-start | bytes 147456
  491.5 299.5 %reduce-scatter.54.cloned.1.call-start = ((), (), s32[]{:S(2)}) async-start(), calls=%async_computation.33 | async-start | bytes 147456
  492.3 354.3 %reduce-scatter.48.cloned.1.call-start = ((), (), s32[]{:S(2)}) async-start(), calls=%async_computation.30 | async-start | bytes 4718592 | tf_op jit(solution)/shard_map/reduce_scatter | solution.py:143
  496.8 1.2 copy-start.16
  496.8 1.9 copy-start.18
  496.9 405.0 %reduce-scatter.50.cloned.1.call-start = ((), (), s32[]{:S(2)}) async-start(), calls=%async_computation.31 | async-start | bytes 4718592 | tf_op jit(solution)/shard_map/reduce_scatter | solution.py:145
  502.3 1.2 copy-start.9
  502.4 439.7 %reduce-scatter.46.cloned.1.call-start = ((), (), s32[]{:S(2)}) async-start(), calls=%async_computation.29 | async-start | bytes 1179648 | tf_op jit(solution)/shard_map/reduce_scatter | solution.py:139
  505.0 487.6 %reduce-scatter.44.cloned.1.call-start = ((), (), s32[]{:S(2)}) async-start(), calls=%async_computation.28 | async-start | bytes 3538944 | tf_op jit(solution)/shard_map/reduce_scatter | solution.py:136
Sparse Core Ops, SparseCore 0:
  54.1 25.7 all-gather.14
  82.3 25.3 all-gather.16
  115.1 44.0 reduce-scatter.35
  161.1 27.1 all-gather.20
  190.4 27.9 all-gather.18
  220.4 27.4 all-gather.24
  249.9 27.6 all-gather.22
  286.6 43.9 reduce-scatter.39
  332.8 43.1 reduce-scatter.37
  379.2 27.2 all-gather.26
  419.7 43.3 reduce-scatter.41
  466.0 33.4 reduce-scatter.65
  502.8 33.3 reduce-scatter.57
  539.1 33.3 reduce-scatter.55
  575.6 33.3 reduce-scatter.63
  611.9 33.3 reduce-scatter.67
  648.4 33.3 reduce-scatter.59
  684.6 33.3 reduce-scatter.61
  721.3 33.3 reduce-scatter.51
  757.6 33.3 reduce-scatter.53
  795.3 51.3 reduce-scatter.47
  850.6 51.2 reduce-scatter.49
  906.0 36.0 reduce-scatter.45
  946.3 46.2 reduce-scatter.43
where the time goes:
time: 1000 us; the launch traced here: 999 us
  waiting for transfers between devices  759 us (76%)
  blocking collectives  119 us (12%)
  matrix products  45.5 us (5%)
  local copies, waits for them, and re-layouts  41.7 us (4%)
  other arithmetic  16.8 us (2%)
  between operations  16.2 us (2%)
    unnamed x33, waiting for transfers between devices  272 us
    reduce_scatter x1, waiting for transfers between devices, spread(): lax.psum_scatter(pieces[11], 'fsdp', scatter_dimension=1, tiled=True)  55.3 us
    reduce_scatter x1, waiting for transfers between devices, spread(): lax.psum_scatter(pieces[9], 'fsdp', scatter_dimension=0, tiled=True)  54.4 us
    reduce_scatter x1, waiting for transfers between devices, spread(): lax.psum_scatter(pieces[2], 'fsdp', scatter_dimension=0, tiled=True)  50.5 us
    reduce_scatter x1, waiting for transfers between devices, forward_pass(): lax.psum_scatter(jnp.dot(act_up, w_down, preferred_element_type=jnp.float...  44.2 us
    reduce_scatter x1, waiting for transfers between devices, spread(): lax.psum_scatter(pieces[5], 'fsdp', scatter_dimension=1, tiled=True)  40.2 us
    reduce_scatter x1, waiting for transfers between devices, backward_pass(): lax.psum_scatter(jnp.dot(grad_qkv_low, qkv_matrix.T, preferred_element_ty...  40 us
    unnamed x85, local copies, waits for them, and re-layouts  34.7 us
  transfers between devices with their start and end apart: 24, of which 23 were waited for; matrix products, arithmetic and copies ran while one was open for 6% of the time, Pallas kernels for 0%

commit v1 on v0

--- a/solution.py
+++ b/solution.py
@@ -6,6 +6,16 @@
 HEAD_DIM = 64
 NORM_EPS = 1e-05
 NEG_FILL = -1e30
+
+
+def turned_line(shard, axis, dim):
+    peers = lax.axis_size(axis)
+    current, shards = (shard, [shard])
+    for _ in range(peers - 1):
+        current = lax.ppermute(current, axis, [(i, (i + 1) % peers) for i in range(peers)])
+        shards.insert(0, current)
+    line = jnp.concatenate(shards, axis=dim)
+    return jnp.roll(line, (lax.axis_index(axis) + 1) * shard.shape[dim], axis=dim)
 
 
 def layer_norm(inputs, norm_gain, norm_shift):
@@ -201,7 +211,7 @@
     hidden_one = tokens_wide + attn_term + proj_bias.astype(jnp.float32)
     normed_mlp = layer_norm(hidden_one, mlp_gain.astype(jnp.float32), mlp_shift.astype(jnp.float32))
     act_mlp = normed_mlp.astype(jnp.bfloat16)
-    mlp_inputs = lax.all_gather(act_mlp, "shard", axis=0, tiled=True)
+    mlp_inputs = turned_line(act_mlp, "shard", 0)
     pre_act = jnp.dot(mlp_inputs, w_up, preferred_element_type=jnp.float32) + up_bias.astype(
         jnp.float32
     )

time: 1000 us -> 970 us (0.970)
  waiting for transfers between devices: 759 us -> 723 us
    all_gather x1 -> x0, waiting for transfers between devices: 30 us -> none  [forward_pass(): mlp_inputs = lax.all_gather(act_mlp, 'shard', axis=0, tiled=True)]
    ppermute x0 -> x3, waiting for transfers between devices: none -> 18 us  [turned_line(): lax.ppermute(current, axis, [(i, (i + 1) % peers) for i in range(peers)])]
    all_gather x1, waiting for transfers between devices: 15.5 us -> 0.01 us  [collect(): lax.all_gather(params[9], 'fsdp', axis=0, tiled=True)]
    unnamed x85 -> x87, local copies, waits for them, and re-layouts: 34.7 us -> 38.5 us
    unnamed x33 -> x32, waiting for transfers between devices: 272 us -> 272 us
  transfers between devices with their start and end apart: 24 -> 26, of which waited for: 23 -> 23; matrix products, arithmetic and copies ran while one was open for 6% -> 6% of each run, Pallas kernels for 0% -> 0%
where the time goes in v1:
time: 970 us; the launch traced here: 968 us
  waiting for transfers between devices  723 us (75%)
  blocking collectives  120 us (12%)
  local copies, waits for them, and re-layouts  45.5 us (5%)
  matrix products  45 us (5%)
  other arithmetic  17.8 us (2%)
  between operations  15.9 us (2%)
    unnamed x32, waiting for transfers between devices  272 us
    reduce_scatter x1, waiting for transfers between devices, spread(): lax.psum_scatter(pieces[11], 'fsdp', scatter_dimension=1, tiled=True)  55.3 us
    reduce_scatter x1, waiting for transfers between devices, spread(): lax.psum_scatter(pieces[9], 'fsdp', scatter_dimension=0, tiled=True)  54.2 us
    reduce_scatter x1, waiting for transfers between devices, spread(): lax.psum_scatter(pieces[2], 'fsdp', scatter_dimension=0, tiled=True)  50.6 us
    reduce_scatter x1, waiting for transfers between devices, forward_pass(): lax.psum_scatter(jnp.dot(act_up, w_down, preferred_element_type=jnp.float...  44.2 us
    reduce_scatter x1, waiting for transfers between devices, spread(): lax.psum_scatter(pieces[5], 'fsdp', scatter_dimension=1, tiled=True)  40.1 us
    reduce_scatter x1, waiting for transfers between devices, backward_pass(): lax.psum_scatter(jnp.dot(grad_qkv_low, qkv_matrix.T, preferred_element_ty...  39.8 us
    unnamed x87, local copies, waits for them, and re-layouts  38.5 us
  transfers between devices with their start and end apart: 26, of which 23 were waited for; matrix products, arithmetic and copies ran while one was open for 6% of the time, Pallas kernels for 0%

profile of v1, /device:TPU:0, one launch (start us, length us, event | category | flops | bytes accessed | tf_op | source)
XLA Modules:
  0.0 968.3 jit_solution(10072573433023956776)
XLA Ops:
  15.9 15.1 %all-reduce.15 = (bf16[256]{0:T(256)(128)(2,1)S(1)}, bf16[256]{0:T(256)(128)(2,1)S(1)}, bf16[256]{0:T(256)(128)(2,1)S(1)}, bf16[256]{0:T(256)(128)(2,1)S(1)}, bf...) all-reduce(bf16[256]{0:T(256)(128)(2,1)S(1)} %dynamic-update-slice., ...), channel_id=1, replica_groups=mesh['fsdp'=8,'shard'=4] {'fsdp'}, use_global_device_ids=true, to_apply=%add.1 | all-reduce | flops 2048 | bytes 8192
  31.1 11.2 %all-gather.1 = bf16[4,1,256]{2,1,0:T(2,128)(2,1)S(1)} all-gather(bf16[1,1,256]{2,1,0:T(2,128)(2,1)S(1)} %reshape.315), channel_id=1, replica_groups=mesh['fsdp'=8,'shard'=4] {'shard'}, dimensions={0}, use_global_device_ids=true | all-gather | bytes 2560 | tf_op jit(solution)/shard_map/all_gather | solution.py:68
  42.2 7.6 all-gather
  55.9 9.7 %all-gather.2 = s32[4,1,128]{2,1,0:T(1,128)S(1)} all-gather(s32[1,1,128]{2,1,0:T(1,128)} %bitcast.156), channel_id=1, replica_groups=mesh['fsdp'=8,'shard'=4] {'shard'}, dimensions={0}, use_global_device_ids=true | all-gather | bytes 2560 | tf_op jit(solution)/shard_map/all_gather | solution.py:186
  65.6 9.0 all_gather.86
  74.7 5.2 all-gather.14.cloned.1.call-done
  79.9 27.8 %all-gather.16.cloned.1.call-done = bf16[1024,3,256]{0,2,1:T(8,128)(2,1)} async-done(((bf16[128,3,256]{0,2,1:T(8,128)(2,1)}), bf16[1024,3,256]{0,2,1:T(8,128)(2,1)}) %all-gather.16.cloned.1.call-update) | async-done | bytes 1572880 | tf_op jit(solution)/shard_map/all_gather | solution.py:54
  107.7 2.7 add_convert_fusion
  117.8 11.1 %all-gather.3 = bf16[4,1,256]{2,1,0:T(2,128)(2,1)S(1)} all-gather(bf16[1,1,256]{2,1,0:T(2,128)(2,1)S(1)} %reshape.319), channel_id=1, replica_groups=mesh['fsdp'=8,'shard'=4] {'shard'}, dimensions={0}, use_global_device_ids=true | all-gather | bytes 2560 | tf_op jit(solution)/shard_map/all_gather | solution.py:69
  128.9 7.6 all-gather.5
  136.5 11.4 %all-gather.4 = bf16[4,1,256]{2,1,0:T(2,128)(2,1)S(1)} all-gather(bf16[1,1,256]{2,1,0:T(2,128)(2,1)S(1)} %reshape.321), channel_id=1, replica_groups=mesh['fsdp'=8,'shard'=4] {'shard'}, dimensions={0}, use_global_device_ids=true | all-gather | bytes 2560 | tf_op jit(solution)/shard_map/all_gather | solution.py:70
  148.0 11.1 %reduce-scatter.36.cloned.1.call-done = f32[128,1024]{1,0:T(8,128)} async-done(((f32[512,1024]{1,0:T(8,128)}), f32[128,1024]{1,0:T(8,128)}) %reduce-scatter.36.cloned.1.call-update) | async-done | bytes 524304 | tf_op jit(solution)/shard_map/reduce_scatter | solution.py:205
  161.2 9.3 collective-permute-done
  170.4 8.7 collective-permute-done.1
  179.2 8.9 all_gather.94
  194.2 4.5 fusion.20
  198.7 19.6 %all-gather.22.cloned.1.call-done = bf16[512,1024]{1,0:T(8,128)(2,1)} async-done(((bf16[128,1024]{1,0:T(8,128)(2,1)}), bf16[512,1024]{1,0:T(8,128)(2,1)}) %all-gather.22.cloned.1.call-update) | async-done | bytes 1048592 | tf_op jit(solution)/shard_map/all_gather | solution.py:266
  218.4 29.6 %all-gather.20.cloned.1.call-done = bf16[1024,1024]{1,0:T(8,128)(2,1)} async-done(((bf16[1024,128]{1,0:T(8,128)(2,1)}), bf16[1024,1024]{1,0:T(8,128)(2,1)}) %all-gather.20.cloned.1.call-update) | async-done | bytes 2097168 | tf_op jit(solution)/shard_map/all_gather | solution.py:63
  248.0 5.2 fusion.69
  254.1 2.6 fusion.36
  256.8 5.1 fusion.67
  262.0 11.1 %all-gather.6 = bf16[4,1,256]{2,1,0:T(2,128)(2,1)S(1)} all-gather(bf16[1,1,256]{2,1,0:T(2,128)(2,1)S(1)} %reshape.325), channel_id=1, replica_groups=mesh['fsdp'=8,'shard'=4] {'shard'}, dimensions={0}, use_global_device_ids=true | all-gather | bytes 2560 | tf_op jit(solution)/shard_map/all_gather | solution.py:72
  273.1 27.7 %reduce-scatter.40.cloned.1.call-done = f32[128,1024]{1,0:T(8,128)} async-done(((f32[512,1024]{1,0:T(8,128)}), f32[128,1024]{1,0:T(8,128)}) %reduce-scatter.40.cloned.1.call-update) | async-done | bytes 524304 | tf_op jit(solution)/shard_map/reduce_scatter | solution.py:275
  302.1 44.2 %reduce-scatter.38.cloned.1.call-done = f32[128,1024]{1,0:T(8,128)} async-done(((f32[512,1024]{1,0:T(8,128)}), f32[128,1024]{1,0:T(8,128)}) %reduce-scatter.38.cloned.1.call-update) | async-done | bytes 524304 | tf_op jit(solution)/shard_map/reduce_scatter | solution.py:219
  346.3 2.1 fusion.71
  349.4 27.4 %all-gather.24.cloned.1.call-done = bf16[512,1024]{1,0:T(8,128)(2,1)} async-done(((bf16[128,1024]{1,0:T(8,128)(2,1)}), bf16[512,1024]{1,0:T(8,128)(2,1)}) %all-gather.24.cloned.1.call-update) | async-done | bytes 1048592 | tf_op jit(solution)/shard_map/all_gather | solution.py:287
  380.5 2.3 fusion.76
  382.8 2.2 fusion.13
  386.4 2.4 fusion.81
  392.4 39.8 %reduce-scatter.42.cloned.1.call-done = f32[128,1024]{1,0:T(8,128)} async-done(((f32[512,1024]{1,0:T(8,128)}), f32[128,1024]{1,0:T(8,128)}) %reduce-scatter.42.cloned.1.call-update) | async-done | bytes 524304 | tf_op jit(solution)/shard_map/reduce_scatter | solution.py:324
  435.0 2.3 fusion.38
  437.3 17.1 %all-reduce.14 = (f32[4,256]{1,0:T(4,128)S(1)}, f32[4,256]{1,0:T(4,128)S(1)}, f32[4,256]{1,0:T(4,128)S(1)}, f32[4,256]{1,0:T(4,128)S(1)}, f32[4,256]{1,0:T(4,128)S(1)}, /*index=5*/f32[4,256]{1,0:T(4,128)S(1)}) all-reduce(f32[4,256]{1,0:T(4,128)S(1)} %reshape.272, ...), channel_id=6, replica_groups=mesh['fsdp'=8,'shard'=4] {'shard'}, use_global_device_ids=true, to_apply=%region_16.17.clone | all-reduce | flops 6144 | bytes 49152
  461.5 4.4 fusion.18
  467.9 3.6 fusion.66
  474.2 2.4 fusion.82
  476.6 2.5 copy.88
  480.6 24.8 %reduce-scatter.56.cloned.1.call-done = f32[32,1]{1,0:T(8,128)} async-done(((f32[256,1]{1,0:T(8,128)}), f32[32,1]{1,0:T(8,128)}) %reduce-scatter.56.cloned.1.call-update) | async-done | bytes 144
  506.7 35.1 %reduce-scatter.58.cloned.1.call-done = f32[32,1]{1,0:T(8,128)} async-done(((f32[256,1]{1,0:T(8,128)}), f32[32,1]{1,0:T(8,128)}) %reduce-scatter.58.cloned.1.call-update) | async-done | bytes 144
  543.1 35.2 %reduce-scatter.52.cloned.1.call-done = f32[32,1]{1,0:T(8,128)} async-done(((f32[256,1]{1,0:T(8,128)}), f32[32,1]{1,0:T(8,128)}) %reduce-scatter.52.cloned.1.call-update) | async-done | bytes 144
  579.6 34.9 %reduce-scatter.54.cloned.1.call-done = f32[32,1]{1,0:T(8,128)} async-done(((f32[256,1]{1,0:T(8,128)}), f32[32,1]{1,0:T(8,128)}) %reduce-scatter.54.cloned.1.call-update) | async-done | bytes 144
  615.8 35.2 %reduce-scatter.60.cloned.1.call-done = f32[32,1]{1,0:T(8,128)} async-done(((f32[256,1]{1,0:T(8,128)}), f32[32,1]{1,0:T(8,128)}) %reduce-scatter.60.cloned.1.call-update) | async-done | bytes 144
  652.4 34.9 %reduce-scatter.62.cloned.1.call-done = f32[32,1]{1,0:T(8,128)} async-done(((f32[256,1]{1,0:T(8,128)}), f32[32,1]{1,0:T(8,128)}) %reduce-scatter.62.cloned.1.call-update) | async-done | bytes 144
  688.6 35.2 %reduce-scatter.64.cloned.1.call-done = f32[32,1]{1,0:T(8,128)} async-done(((f32[256,1]{1,0:T(8,128)}), f32[32,1]{1,0:T(8,128)}) %reduce-scatter.64.cloned.1.call-update) | async-done | bytes 144
  725.1 35.1 %reduce-scatter.68.cloned.1.call-done = f32[32,1]{1,0:T(8,128)} async-done(((f32[256,1]{1,0:T(8,128)}), f32[32,1]{1,0:T(8,128)}) %reduce-scatter.68.cloned.1.call-update) | async-done | bytes 144
  761.5 54.2 %reduce-scatter.48.cloned.1.call-done = f32[128,1024]{1,0:T(8,128)} async-done(((f32[1024,1024]{1,0:T(8,128)}), f32[128,1024]{1,0:T(8,128)}) %reduce-scatter.48.cloned.1.call-update) | async-done | bytes 524304 | tf_op jit(solution)/shard_map/reduce_scatter | solution.py:153
  815.8 55.3 %reduce-scatter.50.cloned.1.call-done = f32[1024,128]{1,0:T(8,128)} async-done(((f32[1024,1024]{1,0:T(8,128)}), f32[1024,128]{1,0:T(8,128)}) %reduce-scatter.50.cloned.1.call-update) | async-done | bytes 524304 | tf_op jit(solution)/shard_map/reduce_scatter | solution.py:155
  871.0 40.1 %reduce-scatter.46.cloned.1.call-done = f32[256,128]{1,0:T(8,128)} async-done(((f32[256,1024]{1,0:T(8,128)}), f32[256,128]{1,0:T(8,128)}) %reduce-scatter.46.cloned.1.call-update) | async-done | bytes 131088 | tf_op jit(solution)/shard_map/reduce_scatter | solution.py:149
  911.2 50.6 %reduce-scatter.44.cloned.1.call-done = f32[128,3,256]{2,0,1:T(8,128)} async-done(((f32[1024,3,256]{2,0,1:T(8,128)}), f32[128,3,256]{2,0,1:T(8,128)}) %reduce-scatter.44.cloned.1.call-update) | async-done | bytes 393232 | tf_op jit(solution)/shard_map/reduce_scatter | solution.py:146
  (202 shorter events, 67.1 us)
Async XLA Ops:
  7.2 58.4 %copy-start.8 = (bf16[256,128]{1,0:T(8,128)(2,1)S(1)}, bf16[256,128]{1,0:T(8,128)(2,1)}, u32[]{:S(2)}) copy-start(bf16[256,128]{1,0:T(8,128)(2,1)} %param.26) | copy-start | bytes 196612
  7.2 72.7 %all-gather.14.cloned.1.call-start = ((), (), s32[]{:S(2)}) async-start(), calls=%async_computation.17 | async-start | bytes 1310720 | tf_op jit(solution)/shard_map/all_gather | solution.py:185
  54.0 53.7 %all-gather.16.cloned.1.call-start = ((), (), s32[]{:S(2)}) async-start(), calls=%async_computation.18 | async-start | bytes 1769472 | tf_op jit(solution)/shard_map/all_gather | solution.py:54
  55.8 103.3 %reduce-scatter.36.cloned.1.call-start = ((), (), s32[]{:S(2)}) async-start(), calls=%async_computation.19 | async-start | bytes 2621440 | tf_op jit(solution)/shard_map/reduce_scatter | solution.py:205
  74.6 38.6 %copy-start.3 = (bf16[256,1024]{1,0:T(8,128)(2,1)}, bf16[256,1024]{1,0:T(8,128)(2,1)S(1)}, u32[]{:S(2)}) copy-start(bf16[256,1024]{1,0:T(8,128)(2,1)S(1)} %all_gather.86) | copy-start | bytes 1572868
  111.6 1.1 copy-start.4
  112.1 0.9 copy-start.6
  113.2 3.1 copy-start.2
  115.0 44.1 %copy-start = (bf16[128,1024]{1,0:T(8,128)(2,1)S(1)}, bf16[128,1024]{1,0:T(8,128)(2,1)}, u32[]{:S(2)}) copy-start(bf16[128,1024]{1,0:T(8,128)(2,1)} %param.17) | copy-start | bytes 786436
  115.0 64.1 %copy-start.9 = (bf16[1,128]{1,0:T(2,128)(2,1)S(1)}, bf16[1,128]{1,0:T(2,128)(2,1)}, u32[]{:S(2)}) copy-start(bf16[1,128]{1,0:T(2,128)(2,1)} %param.31) | copy-start | bytes 772
  115.1 79.2 %all-gather.18.cloned.1.call-start = ((), (), s32[]{:S(2)}) async-start(), calls=%async_computation.20 | async-start | bytes 2359296 | tf_op jit(solution)/shard_map/all_gather | solution.py:61
  115.6 102.7 %all-gather.22.cloned.1.call-start = ((), (), s32[]{:S(2)}) async-start(), calls=%async_computation.23 | async-start | bytes 1310720 | tf_op jit(solution)/shard_map/all_gather | solution.py:266
  117.2 130.8 %all-gather.20.cloned.1.call-start = ((), (), s32[]{:S(2)}) async-start(), calls=%async_computation.21 | async-start | bytes 2359296 | tf_op jit(solution)/shard_map/all_gather | solution.py:63
  117.8 183.1 %reduce-scatter.40.cloned.1.call-start = ((), (), s32[]{:S(2)}) async-start(), calls=%async_computation.24 | async-start | bytes 2621440 | tf_op jit(solution)/shard_map/reduce_scatter | solution.py:275
  160.7 9.7 %collective-permute-start = (bf16[128,1024]{1,0:T(8,128)(2,1)S(1)}, bf16[128,1024]{1,0:T(8,128)(2,1)S(1)}, u32[]{:S(2)}, u32[]{:S(2)}) collective-permute-start(bf16[128,1024]{1,0:T(8,128)(2,1)S(1)} %add_convert_fusion.1), channel_id=1, source_target_pairs={{0,1},{1,2},{2,3},{3,0},{4,5},{5,6},{6,7},{7,4},{8,9},{9,10},{10,1... | collective-permute-start | bytes 786440 | tf_op jit(solution)/shard_map/ppermute | solution.py:15
  170.4 8.7 collective-permute-start.1
  179.2 8.9 collective-permute-start.2
  248.0 6.2 copy-start.10
  253.2 1.0 copy-start.14
  256.7 89.6 %reduce-scatter.38.cloned.1.call-start = ((), (), s32[]{:S(2)}) async-start(), calls=%async_computation.22 | async-start | bytes 2621440 | tf_op jit(solution)/shard_map/reduce_scatter | solution.py:219
  261.9 114.9 %all-gather.24.cloned.1.call-start = ((), (), s32[]{:S(2)}) async-start(), calls=%async_computation.25 | async-start | bytes 1310720 | tf_op jit(solution)/shard_map/all_gather | solution.py:287
  349.3 82.9 %reduce-scatter.42.cloned.1.call-start = ((), (), s32[]{:S(2)}) async-start(), calls=%async_computation.26 | async-start | bytes 2621440 | tf_op jit(solution)/shard_map/reduce_scatter | solution.py:324
  379.1 3.7 copy-start.5
  385.0 1.4 copy-start.11
  386.4 2.4 copy-start.1
  388.7 2.0 copy-start.13
  388.7 90.4 %reduce-scatter.66.cloned.1.call-start = ((), (), s32[]{:S(2)}) async-start(), calls=%async_computation.38 | async-start | bytes 589824
  389.8 115.5 %reduce-scatter.56.cloned.1.call-start = ((), (), s32[]{:S(2)}) async-start(), calls=%async_computation.33 | async-start | bytes 147456
  390.7 151.1 %reduce-scatter.58.cloned.1.call-start = ((), (), s32[]{:S(2)}) async-start(), calls=%async_computation.34 | async-start | bytes 147456
  392.2 186.1 %reduce-scatter.52.cloned.1.call-start = ((), (), s32[]{:S(2)}) async-start(), calls=%async_computation.31 | async-start | bytes 147456
  434.9 26.6 %copy-start.15 = (bf16[512,1024]{1,0:T(8,128)(2,1)S(1)}, bf16[512,1024]{1,0:T(8,128)(2,1)}, u32[]{:S(2)}) copy-start(bf16[512,1024]{1,0:T(8,128)(2,1)} %copy-done.14) | copy-start | bytes 3145732
  455.8 158.8 %reduce-scatter.54.cloned.1.call-start = ((), (), s32[]{:S(2)}) async-start(), calls=%async_computation.32 | async-start | bytes 147456
  456.6 194.4 %reduce-scatter.60.cloned.1.call-start = ((), (), s32[]{:S(2)}) async-start(), calls=%async_computation.35 | async-start | bytes 147456
  458.2 229.1 %reduce-scatter.62.cloned.1.call-start = ((), (), s32[]{:S(2)}) async-start(), calls=%async_computation.36 | async-start | bytes 147456
  459.0 264.8 %reduce-scatter.64.cloned.1.call-start = ((), (), s32[]{:S(2)}) async-start(), calls=%async_computation.37 | async-start | bytes 147456
  460.6 299.6 %reduce-scatter.68.cloned.1.call-start = ((), (), s32[]{:S(2)}) async-start(), calls=%async_computation.39 | async-start | bytes 147456
  461.5 354.3 %reduce-scatter.48.cloned.1.call-start = ((), (), s32[]{:S(2)}) async-start(), calls=%async_computation.29 | async-start | bytes 4718592 | tf_op jit(solution)/shard_map/reduce_scatter | solution.py:153
  466.0 1.2 copy-start.12
  466.0 1.9 copy-start.16
  466.0 405.0 %reduce-scatter.50.cloned.1.call-start = ((), (), s32[]{:S(2)}) async-start(), calls=%async_computation.30 | async-start | bytes 4718592 | tf_op jit(solution)/shard_map/reduce_scatter | solution.py:155
  471.4 1.2 copy-start.7
  471.5 439.7 %reduce-scatter.46.cloned.1.call-start = ((), (), s32[]{:S(2)}) async-start(), calls=%async_computation.28 | async-start | bytes 1179648 | tf_op jit(solution)/shard_map/reduce_scatter | solution.py:149
  474.1 487.6 %reduce-scatter.44.cloned.1.call-start = ((), (), s32[]{:S(2)}) async-start(), calls=%async_computation.27 | async-start | bytes 3538944 | tf_op jit(solution)/shard_map/reduce_scatter | solution.py:146
Sparse Core Ops, SparseCore 0:
  54.1 25.7 all-gather.13
  82.3 25.3 all-gather.15
  115.2 43.9 reduce-scatter.35
  161.0 27.2 all-gather.17
  190.4 27.9 all-gather.21
  220.3 27.6 all-gather.19
  256.9 43.9 reduce-scatter.39
  303.1 43.1 reduce-scatter.37
  349.5 27.2 all-gather.23
  388.9 43.3 reduce-scatter.41
  435.4 33.4 reduce-scatter.65
  472.0 33.3 reduce-scatter.55
  508.4 33.3 reduce-scatter.57
  544.9 33.3 reduce-scatter.51
  581.1 33.3 reduce-scatter.53
  617.7 33.3 reduce-scatter.59
  653.9 33.3 reduce-scatter.61
  690.4 33.3 reduce-scatter.63
  726.8 33.3 reduce-scatter.67
  764.4 51.3 reduce-scatter.47
  819.7 51.2 reduce-scatter.49
  875.1 36.0 reduce-scatter.45
  915.5 46.2 reduce-scatter.43
